TPU v7x, 32 devices: a whole 2x2x4 slice. The times are simulated.
32 devices in a mesh: az: 16 (over z, x, core), dep: 2 (over y).
Axes of the slice: x: 2, y: 2, z: 4, core: 2. Of those that a mesh axis runs over, the one named last changes fastest.
Arguments:
- field: float32 [1024, 2, 1024], P('az', None, 'dep'), may hold values from -6 to 6
- brick_speed: bfloat16 [4096, 1024], P('az', 'dep'), may hold values from -40 to 40
- send_index: int32 [16, 16, 32], P('az'), may hold values from 0 to 255
- send_count: int32 [16, 16], P('az'), may hold values from 0 to 32, as said below
- weights: bfloat16 [1024, 4, 512], P('az'), may hold values from 0 to 1, as said below
- propagator: bfloat16 [2, 2, 1024, 1024], replicated, may hold values from -1 to 1
Outputs:
- pressure: float32 [1024, 2, 1024], P('az', None, 'dep')
Inputs may be any that keep to these rules, and one draw needn't show every extreme that they name: `send_count`: 32 or fewer columns from one brick to one sector; one sector receives 32 from every brick. Nonnegative interpolation weights.
All inputs are finite; a program needn't handle non-finite values.
Results may differ from a plain program's by a relative error of at most 0.025.
Values may be sent and summed in bfloat16 or wider, within the bound.
A program may use at most 64 MiB of HBM per device.

v0:
```python
import functools
import math

import jax
import jax.numpy as jnp
from jax import lax
from jax.experimental import pallas as pl
from jax.experimental.pallas import tpu as pltpu
from jax.sharding import PartitionSpec as P

angle_rate = 200.0 / 1500.0
couple_real = 0.1
couple_imag = 0.15
MESH = pl.DeviceIdType.MESH
LANES = 128


def sine_cosine(x):
    turns = jnp.floor(x * (2.0 / math.pi) + 0.5)
    r = x - turns * 1.5703125
    r = r - turns * 4.837512969970703125e-4
    r = r - turns * 7.549789948768648e-8
    quadrant = turns.astype(jnp.int32)
    r2 = r * r
    sine = r + r * r2 * (-1.0 / 6.0 + r2 * (1.0 / 120.0 + r2 * (-1.0 / 5040.0)))
    cosine = 1.0 + r2 * (-0.5 + r2 * (1.0 / 24.0 + r2 * (-1.0 / 720.0 + r2 * (1.0 / 40320.0))))
    swap = (quadrant & 1) == 1
    out_sine = jnp.where(swap, cosine, sine)
    out_cosine = jnp.where(swap, sine, cosine)
    out_sine = jnp.where((quadrant & 2) == 2, -out_sine, out_sine)
    out_cosine = jnp.where(((quadrant + 1) & 2) == 2, -out_cosine, out_cosine)
    return out_sine, out_cosine


def march_kernel(
    n, steps, factors, cap, halo, half,
    field_hbm, brick_hbm, index_hbm, count_hbm, weights_hbm, prop_ref,
    out_ref,
    field_ref, brick_ref, index_ref, count_ref, weights_ref, out_r,
    prop, step_prop, rows_f, packed, recv, mixw, angles,
    fpeer_s, fpeer_r, fhalo_s, fhalo_r,
    apeer_s, apeer_r, ahalo_s, ahalo_r,
    sines, cosines, state, out_s,
    load_sem, prop_sem, pp_ss, pp_rs, a2a_ss, a2a_rs, fp_sem, fh_ss, fh_rs, ap_ss, ap_rs, ah_ss, ah_rs, out_sem,
):
    i = lax.axis_index("az")
    j = lax.axis_index("dep")
    other = 1 - j
    h = lax.rem(i + j, 2)
    first = h == 0
    rows = 2 * half
    whole = prop.shape[2]
    block_rows = LANES
    share = lax.rem(i, 2)
    twin = i + 1 - 2 * share
    window = half + 2 * halo
    wide = half + 2 * halo
    shift = rows - wide
    chunks = packed.shape[0]
    depth = brick_ref.shape[1]
    bcol = brick_ref.shape[0]
    before = lax.rem(i + n - 1, n)
    after = lax.rem(i + 1, n)
    before_dep = lax.rem(i, 2)
    after_dep = 1 - before_dep

    barrier = pltpu.get_barrier_semaphore()

    def greet(q, carry):
        pl.semaphore_signal(
            barrier, inc=1, device_id=(lax.rem(i + 1 + q, n), j), device_id_type=MESH
        )
        return carry

    lax.fori_loop(0, n - 1, greet, 0)
    for target in (i, before, after):
        pl.semaphore_signal(barrier, inc=1, device_id=(target, other), device_id_type=MESH)

    loads = []
    for q, (src, dst) in enumerate(
        (
            (index_hbm, index_ref),
            (count_hbm, count_ref),
            (brick_hbm, brick_ref),
            (field_hbm, field_ref),
            (weights_hbm, weights_ref),
        )
    ):
        load = pltpu.make_async_copy(src, dst, load_sem.at[q])
        load.start()
        loads.append(load)
    fetches = []
    for f in range(factors):
        fetch = pltpu.make_async_copy(prop_ref.at[f], prop.at[f], prop_sem.at[f])
        fetch.start()
        fetches.append(fetch)

    for load in loads[0:3]:
        load.wait()
    slots = lax.broadcasted_iota(jnp.int32, (cap, n), 0)
    chosen = jnp.transpose(index_ref[0], (1, 0))
    chosen = jnp.where(slots < count_ref[...], chosen, -1)
    column = lax.broadcasted_iota(jnp.int32, (cap, bcol), 1)
    brick = brick_ref[...]
    group = min(n, 8)
    for g in range(n // group):
        onehot = jnp.concatenate(
            [
                (column == chosen[:, d : d + 1]).astype(jnp.float32).astype(jnp.bfloat16)
                for d in range(g * group, (g + 1) * group)
            ],
            axis=0,
        )
        picked = jnp.dot(onehot, brick, preferred_element_type=jnp.float32).astype(jnp.bfloat16)
        for c in range(chunks):
            packed[c, g * group : (g + 1) * group] = picked[
                :, c * LANES : (c + 1) * LANES
            ].reshape(group, cap, LANES)

    pl.semaphore_wait(barrier, n + 2)

    for c in range(chunks):

        def send(q, carry):
            target = lax.rem(i + 1 + lax.rem(q + n // 2 - 1, n - 1), n)
            pltpu.make_async_remote_copy(
                src_ref=packed.at[c, target],
                dst_ref=recv.at[c, i],
                send_sem=a2a_ss.at[c],
                recv_sem=a2a_rs.at[c],
                device_id=(target, j),
                device_id_type=MESH,
            ).start()
            return carry

        lax.fori_loop(0, n - 1, send, 0)
        recv[c, i] = packed[c, i]

    loads[3].wait()

    def strided(ref, start, stride):
        return jnp.concatenate(
            [ref[c, pl.ds(start, rows, stride=stride), :] for c in range(ref.shape[0])], axis=1
        )

    def field_part(p):
        return jnp.concatenate(
            [
                field_ref[pl.ds(2 * c + p, rows, stride=2 * chunks), :]
                for c in range(chunks)
            ],
            axis=1,
        )

    parts = [field_part(p) for p in range(2)]
    for p in range(2):
        x = parts[p]
        fpeer_s[p] = jnp.where(first, x[shift:rows], x[0:wide]).astype(jnp.bfloat16)
    fhalo_s[0] = jnp.concatenate([parts[0][0:halo], parts[1][0:halo]], axis=0).astype(jnp.bfloat16)
    fhalo_s[1] = jnp.concatenate(
        [parts[0][rows - halo : rows], parts[1][rows - halo : rows]], axis=0
    ).astype(jnp.bfloat16)

    def remote(src, dst, send_sem, recv_sem, target):
        return pltpu.make_async_remote_copy(
            src_ref=src, dst_ref=dst, send_sem=send_sem, recv_sem=recv_sem,
            device_id=target, device_id_type=MESH,
        )

    def local_wait(ref, sem):
        pltpu.make_async_copy(ref, ref, sem).wait()

    pending = []
    copy = remote(fpeer_s, fpeer_r, fp_sem.at[0], fp_sem.at[1], (i, other))
    copy.start()
    pending.append((fpeer_s, fp_sem.at[0]))
    remote(fhalo_s.at[0], fhalo_r.at[j], fh_ss.at[0], fh_rs.at[j], (before, before_dep)).start()
    remote(fhalo_s.at[1], fhalo_r.at[j], fh_ss.at[1], fh_rs.at[j], (after, after_dep)).start()
    pending.append((fhalo_s.at[0], fh_ss.at[0]))
    pending.append((fhalo_s.at[1], fh_ss.at[1]))

    loads[4].wait()
    for a in range(rows):
        block = weights_ref[a].astype(jnp.float32)
        for c in range(n * cap // LANES):
            rows_f[c, steps * a : steps * (a + 1), :] = block[:, c * LANES : (c + 1) * LANES]
    for k in range(steps):
        mixw[k * rows : (k + 1) * rows, :] = strided(rows_f, k, steps).astype(jnp.bfloat16)

    def windowed(body, edge, low):
        return jnp.where(
            first,
            jnp.concatenate([edge, body[0 : half + halo]], axis=0),
            jnp.concatenate([body[low : low + half + halo], edge], axis=0),
        )

    def finish(c):
        cols = pl.ds(c * LANES, LANES)
        local_wait(apeer_r.at[c], ap_rs.at[c])
        for side in range(2):
            local_wait(ahalo_r.at[c, side], ah_rs.at[c, side])
        edge_own = ahalo_r[c, j].astype(jnp.float32)
        edge_other = ahalo_r[c, other].astype(jnp.float32)
        for k in range(steps):
            own = windowed(
                angles[c, k * rows : (k + 1) * rows, :],
                edge_own[k * halo : (k + 1) * halo],
                rows - half - halo,
            )
            s, co = sine_cosine(own)
            sines[k, j, :, cols] = s
            cosines[k, j, :, cols] = co
            far = windowed(
                apeer_r[c, k].astype(jnp.float32),
                edge_other[k * halo : (k + 1) * halo],
                wide - half - halo,
            )
            s, co = sine_cosine(far)
            sines[k, other, :, cols] = s
            cosines[k, other, :, cols] = co

    def operand(re, im):
        re = re.astype(jnp.bfloat16)
        im = im.astype(jnp.bfloat16)
        left = jnp.concatenate([re, im], axis=0)
        right = jnp.concatenate([-im, re], axis=0)
        return jnp.concatenate([left, right], axis=1)

    def compose(b):
        at = pl.multiple_of(share * (whole // 2) + b * block_rows, block_rows)
        span = pl.ds(at, block_rows)
        re = prop[0, span, :]
        im = prop[0, pl.ds(whole + at, block_rows), :]
        for f in range(1, factors):
            mixed = jnp.dot(operand(re, im), prop[f], preferred_element_type=jnp.float32)
            re, im = mixed[0:block_rows], mixed[block_rows : 2 * block_rows]
        step_prop[0, span, :] = re.astype(jnp.bfloat16)
        step_prop[1, span, :] = im.astype(jnp.bfloat16)
        piece = step_prop.at[:, span, :]
        remote(piece, piece, pp_ss.at[b], pp_rs.at[b], (twin, j)).start()
        pending.append((piece, pp_ss.at[b]))

    for fetch in fetches:
        fetch.wait()
    blocks = pp_ss.shape[0]
    for c in range(chunks):
        for b in range(min(c * blocks // 2, blocks), min((c + 1) * blocks // 2, blocks)):
            compose(b)
        local_wait(recv.at[c, pl.ds(0, n - 1)], a2a_rs.at[c])
        flat = recv[c].reshape(n * cap, LANES)
        speed = jnp.dot(mixw[...], flat, preferred_element_type=jnp.float32)
        angle = -angle_rate * speed
        angles[c] = angle
        heads, tails = [], []
        for k in range(steps):
            x = angle[k * rows : (k + 1) * rows]
            apeer_s[c, k] = jnp.where(first, x[shift:rows], x[0:wide]).astype(jnp.bfloat16)
            heads.append(x[0:halo])
            tails.append(x[rows - halo : rows])
        ahalo_s[c, 0] = jnp.concatenate(heads, axis=0).astype(jnp.bfloat16)
        ahalo_s[c, 1] = jnp.concatenate(tails, axis=0).astype(jnp.bfloat16)
        remote(
            ahalo_s.at[c, 0], ahalo_r.at[c, j], ah_ss.at[c, 0], ah_rs.at[c, j],
            (before, before_dep),
        ).start()
        remote(
            ahalo_s.at[c, 1], ahalo_r.at[c, j], ah_ss.at[c, 1], ah_rs.at[c, j],
            (after, after_dep),
        ).start()
        remote(apeer_s.at[c], apeer_r.at[c], ap_ss.at[c], ap_rs.at[c], (i, other)).start()
        pending.append((ahalo_s.at[c, 0], ah_ss.at[c, 0]))
        pending.append((ahalo_s.at[c, 1], ah_ss.at[c, 1]))
        pending.append((apeer_s.at[c], ap_ss.at[c]))
    local_wait(fpeer_r, fp_sem.at[1])
    for side in range(2):
        local_wait(fhalo_r.at[side], fh_rs.at[side])
    edges = [fhalo_r[j].astype(jnp.float32), fhalo_r[other].astype(jnp.float32)]
    for p in range(2):
        part = field_part(p).astype(jnp.bfloat16).astype(jnp.float32)
        state[p, j] = windowed(
            part, edges[0][p * halo : (p + 1) * halo], rows - half - halo
        )
        state[p, other] = windowed(
            fpeer_r[p].astype(jnp.float32),
            edges[1][p * halo : (p + 1) * halo],
            wide - half - halo,
        )
    for c in range(chunks):
        finish(c)
    for b in range(blocks):
        at = pl.multiple_of((1 - share) * (whole // 2) + b * block_rows, block_rows)
        local_wait(step_prop.at[:, pl.ds(at, block_rows), :], pp_rs.at[b])
    def laplace(x):
        one = pltpu.roll(x, 1, 0) + pltpu.roll(x, window - 1, 0)
        two = pltpu.roll(x, 2, 0) + pltpu.roll(x, window - 2, 0)
        return (16.0 * one - 30.0 * x - two) * (1.0 / 12.0)

    def couple(k):
        tops, lows = [], []
        for side in range(2):
            re, im = state[0, side], state[1, side]
            co, si = cosines[k, side], sines[k, side]
            sre = re * co - im * si
            sim = re * si + im * co
            lre, lim = laplace(sre), laplace(sim)
            tops.append(sre + couple_real * lre - couple_imag * lim)
            lows.append(sim + couple_real * lim + couple_imag * lre)
        return jnp.concatenate(tops, axis=1), jnp.concatenate(lows, axis=1)

    def march(k, carry):
        re, im = couple(k)
        mixed = jnp.dot(operand(re, im), step_prop[...].reshape(2 * whole, whole), preferred_element_type=jnp.float32)
        re, im = mixed[0:window], mixed[window : 2 * window]
        for side in range(2):
            state[0, side] = re[:, side * depth : (side + 1) * depth]
            state[1, side] = im[:, side * depth : (side + 1) * depth]
        return carry

    lax.fori_loop(0, steps - 1, march, 0)

    def put(block, p, x):
        start = block * (half * 2 * chunks)
        for c in range(chunks):
            out_ref[pl.ds(start + 2 * c + p, half, stride=2 * chunks), :] = x[
                :, c * LANES : (c + 1) * LANES
            ]

    re, im = couple(steps - 1)
    both = operand(re, im)

    def last(side):
        columns = pl.ds(pl.multiple_of(side * depth, LANES), depth)
        mixed = jnp.dot(
            both, step_prop[:, :, columns].reshape(2 * whole, depth), preferred_element_type=jnp.float32
        )
        return [mixed[p * window + halo : p * window + halo + half] for p in range(2)]

    ready = last(other)
    for p in range(2):
        out_s[p] = ready[p].astype(jnp.bfloat16)
    remote(out_s, out_r, out_sem.at[0], out_sem.at[1], (i, other)).start()
    ready = last(j)
    for p in range(2):
        put(h, p, ready[p])

    for c in range(chunks):
        local_wait(packed.at[c, pl.ds(0, n - 1)], a2a_ss.at[c])
    for ref, sem in pending:
        local_wait(ref, sem)
    local_wait(out_s, out_sem.at[0])
    local_wait(out_r, out_sem.at[1])
    for p in range(2):
        put(1 - h, p, out_r[p].astype(jnp.float32))


def per_device(field, brick_speed, send_index, send_count, weights, propagator):
    n = lax.axis_size("az")
    rows, _, depth = field.shape
    steps = weights.shape[1]
    factors, _, whole, _ = propagator.shape
    cap = send_index.shape[2]
    half = rows // 2
    halo = 2 * steps
    window = half + 2 * halo
    wide = half + 2 * halo
    chunks = depth // LANES
    merged = propagator.reshape(factors, 2 * whole, whole)
    flat_field = field.reshape(rows, 2, chunks, LANES).transpose(0, 2, 1, 3).reshape(-1, LANES)
    bf16, f32 = jnp.bfloat16, jnp.float32
    dma = pltpu.SemaphoreType.DMA
    vmem = pl.BlockSpec(memory_space=pltpu.VMEM)
    out = pl.pallas_call(
        functools.partial(march_kernel, n, steps, factors, cap, halo, half),
        out_shape=jax.ShapeDtypeStruct(flat_field.shape, f32),
        in_specs=[pl.BlockSpec(memory_space=pl.ANY)] * 6,
        out_specs=vmem,
        scratch_shapes=[
            pltpu.VMEM(flat_field.shape, f32),
            pltpu.VMEM(brick_speed.shape, bf16),
            pltpu.VMEM(send_index.shape, jnp.int32),
            pltpu.VMEM(send_count.shape, jnp.int32),
            pltpu.VMEM(weights.shape, bf16),
            pltpu.VMEM((2, half, depth), bf16),
            pltpu.VMEM((factors, 2 * whole, whole), bf16),
            pltpu.VMEM((2, whole, whole), bf16),
            pltpu.VMEM((n * cap // LANES, rows * steps, LANES), f32),
            pltpu.VMEM((chunks, n, cap, LANES), bf16),
            pltpu.VMEM((chunks, n, cap, LANES), bf16),
            pltpu.VMEM((rows * steps, n * cap), bf16),
            pltpu.VMEM((chunks, rows * steps, LANES), f32),
            pltpu.VMEM((2, wide, depth), bf16),
            pltpu.VMEM((2, wide, depth), bf16),
            pltpu.VMEM((2, 2 * halo, depth), bf16),
            pltpu.VMEM((2, 2 * halo, depth), bf16),
            pltpu.VMEM((chunks, steps, wide, LANES), bf16),
            pltpu.VMEM((chunks, steps, wide, LANES), bf16),
            pltpu.VMEM((chunks, 2, steps * halo, LANES), bf16),
            pltpu.VMEM((chunks, 2, steps * halo, LANES), bf16),
            pltpu.VMEM((steps, 2, window, depth), f32),
            pltpu.VMEM((steps, 2, window, depth), f32),
            pltpu.VMEM((2, 2, window, depth), f32),
            pltpu.VMEM((2, half, depth), bf16),
            dma((5,)),
            dma((factors,)),
            dma((whole // 2 // LANES,)),
            dma((whole // 2 // LANES,)),
            dma((chunks,)),
            dma((chunks,)),
            dma((2,)),
            dma((2,)),
            dma((2,)),
            dma((chunks,)),
            dma((chunks,)),
            dma((chunks, 2)),
            dma((chunks, 2)),
            dma((2,)),
        ],
        compiler_params=pltpu.CompilerParams(collective_id=0, has_side_effects=True),
    )(flat_field, brick_speed, send_index, send_count, weights, merged)
    return out.reshape(rows, chunks, 2, LANES).transpose(0, 2, 1, 3).reshape(rows, 2, depth)


def solution(mesh):
    placed = (
        P("az", None, "dep"),
        P("az", "dep"),
        P("az", None, None),
        P("az", None),
        P("az", None, None),
        P(),
    )
    return jax.shard_map(
        per_device, mesh=mesh, in_specs=placed, out_specs=P("az", None, "dep"), check_vma=False
    )
```

profile of v0, /device:TPU:0, one launch (start us, length us, event | category | flops | bytes accessed | tf_op | source)
XLA Modules:
  0.0 33.3 jit_solution(10572258418622372045)
XLA Ops:
  0.0 31.6 %shard_map.64 = f32[512,128]{1,0:T(8,128)} custom-call(f32[512,128]{1,0:T(8,128)} %bitcast.13, bf16[256,512]{1,0:T(8,128)(2,1)} %brick_hbm.1, s32[1,16,32]{2,1,0:T(8,128)} %index_hbm.1, s32[1,16]{1,0:T(1,128)} %count_hbm.1, bf16[64,4,512]{2,1,0:T(4,128)(2,1)} %weights_hbm.1, bf16[2,2048,1024]{2,1,0:T(8,128)(2,1)} %bitcast.11), custom_call_target="tpu_custom_call" | custom-call | tf_op jit(solution)/shard_map/pallas_call | solution.py:372
  31.6 1.7 %copy.10 = f32[64,2,512]{2,1,0:T(2,128)} copy(f32[64,2,512]{2,1,0:T(2,128)} %bitcast.12) | data formatting | bytes 524288
where the time goes:
time: 33.5 us; the launch traced here: 33.3 us
  Pallas kernels  31.6 us (94%)
  local copies, waits for them, and re-layouts  1.67 us (5%)
    pallas_call x1, Pallas kernels, per_device(): pl.pallas_call(functools.partial(march_kernel, n, steps, factors, cap, ha...  31.6 us
    unnamed x1, local copies, waits for them, and re-layouts  1.67 us

commit v1 on v0

--- a/solution.py
+++ b/solution.py
@@ -46,7 +46,7 @@
     i = lax.axis_index("az")
     j = lax.axis_index("dep")
     other = 1 - j
-    h = lax.rem(i + j, 2)
+    h = lax.rem(i + j + 1, 2)
     first = h == 0
     rows = 2 * half
     whole = prop.shape[2]
@@ -61,8 +61,8 @@
     bcol = brick_ref.shape[0]
     before = lax.rem(i + n - 1, n)
     after = lax.rem(i + 1, n)
-    before_dep = lax.rem(i, 2)
-    after_dep = 1 - before_dep
+    after_dep = lax.rem(i, 2)
+    before_dep = 1 - after_dep
 
     barrier = pltpu.get_barrier_semaphore()
 
@@ -119,21 +119,47 @@
 
     pl.semaphore_wait(barrier, n + 2)
 
+    planes = 4 if n % 4 == 0 else 1
+    plane = n // planes
+    mine = lax.div(i, plane)
+    spot = lax.rem(i, plane)
+    if planes == 4:
+        upper = lax.div(mine, 2)
+        order = (3 - 3 * upper, 2 - upper, mine + 1 - 2 * lax.rem(mine, 2), mine)
+    else:
+        order = (mine,)
+
+    def send(c, target):
+        pltpu.make_async_remote_copy(
+            src_ref=packed.at[c, target],
+            dst_ref=recv.at[c, i],
+            send_sem=a2a_ss.at[c],
+            recv_sem=a2a_rs.at[c],
+            device_id=(target, j),
+            device_id_type=MESH,
+        ).start()
+
     for c in range(chunks):
 
-        def send(q, carry):
-            target = lax.rem(i + 1 + lax.rem(q + n // 2 - 1, n - 1), n)
-            pltpu.make_async_remote_copy(
-                src_ref=packed.at[c, target],
-                dst_ref=recv.at[c, i],
-                send_sem=a2a_ss.at[c],
-                recv_sem=a2a_rs.at[c],
-                device_id=(target, j),
-                device_id_type=MESH,
-            ).start()
-            return carry
-
-        lax.fori_loop(0, n - 1, send, 0)
+        @pl.when(i != n - 1)
+        def _():
+            for ahead in (2 * c, 2 * c + 1):
+                if ahead < chunks:
+                    send(ahead, n - 1)
+
+        for p, there in enumerate(order):
+            own = p == planes - 1
+
+            def spread(q, carry, there=there, own=own):
+                target = there * plane + lax.rem(spot + q + own, plane)
+
+                @pl.when(target != n - 1)
+                def _():
+                    send(c, target)
+
+                return carry
+
+            lax.fori_loop(0, plane - own, spread, 0)
         recv[c, i] = packed[c, i]
 
     loads[3].wait()
@@ -371,7 +397,7 @@
     vmem = pl.BlockSpec(memory_space=pltpu.VMEM)
     out = pl.pallas_call(
         functools.partial(march_kernel, n, steps, factors, cap, halo, half),
-        out_shape=jax.ShapeDtypeStruct(flat_field.shape, f32),
+        out_shape=pltpu.VMEM(flat_field.shape, f32),
         in_specs=[pl.BlockSpec(memory_space=pl.ANY)] * 6,
         out_specs=vmem,
         scratch_shapes=[

time: 33.5 us -> 31.4 us (0.937)
  Pallas kernels: 31.6 us -> 30.5 us
  local copies, waits for them, and re-layouts: 1.67 us -> 0.71 us
    pallas_call x1, Pallas kernels: 31.6 us -> 30.5 us  [per_device(): pl.pallas_call(functools.partial(march_kernel, n, steps, factors, cap, ha...]
    unnamed x1, local copies, waits for them, and re-layouts: 1.67 us -> 0.71 us
where the time goes in v1:
time: 31.4 us; the launch traced here: 31.2 us
  Pallas kernels  30.5 us (97%)
  local copies, waits for them, and re-layouts  0.71 us (2%)
    pallas_call x1, Pallas kernels, per_device(): pl.pallas_call(functools.partial(march_kernel, n, steps, factors, cap, ha...  30.5 us
    unnamed x1, local copies, waits for them, and re-layouts  0.71 us

profile of v1, /device:TPU:0, one launch (start us, length us, event | category | flops | bytes accessed | tf_op | source)
XLA Modules:
  0.0 31.2 jit_solution(17321435042867589872)
XLA Ops:
  0.0 30.5 %shard_map.64 = f32[512,128]{1,0:T(8,128)S(1)} custom-call(f32[512,128]{1,0:T(8,128)} %bitcast.13, bf16[256,512]{1,0:T(8,128)(2,1)} %brick_hbm.1, s32[1,16,32]{2,1,0:T(8,128)} %index_hbm.1, s32[1,16]{1,0:T(1,128)} %count_hbm.1, bf16[64,4,512]{2,1,0:T(4,128)(2,1)} %weights_hbm.1, bf16[2,2048,1024]{2,1,0:T(8,128)(2,1)} %bitcast.12), custom_call_target="tpu_custom_call" | custom-call | tf_op jit(solution)/shard_map/pallas_call | solution.py:398
  30.5 0.7 %copy.10 = f32[64,2,512]{2,1,0:T(2,128)} copy(f32[64,2,512]{2,1,0:T(2,128)S(1)} %bitcast.11) | data formatting | bytes 524288

commit v2 on v1

v2 whole, which is shorter than its diff:
```python
import functools
import math

import jax
import jax.numpy as jnp
from jax import lax
from jax.experimental import pallas as pl
from jax.experimental.pallas import tpu as pltpu
from jax.sharding import PartitionSpec as P

angle_rate = 200.0 / 1500.0
couple_real = 0.1
couple_imag = 0.15
MESH = pl.DeviceIdType.MESH
LANES = 128


def sine_cosine(x):
    turns = jnp.floor(x * (2.0 / math.pi) + 0.5)
    r = x - turns * 1.5703125
    r = r - turns * 4.837512969970703125e-4
    r = r - turns * 7.549789948768648e-8
    quadrant = turns.astype(jnp.int32)
    r2 = r * r
    sine = r + r * r2 * (-1.0 / 6.0 + r2 * (1.0 / 120.0 + r2 * (-1.0 / 5040.0)))
    cosine = 1.0 + r2 * (-0.5 + r2 * (1.0 / 24.0 + r2 * (-1.0 / 720.0 + r2 * (1.0 / 40320.0))))
    swap = (quadrant & 1) == 1
    out_sine = jnp.where(swap, cosine, sine)
    out_cosine = jnp.where(swap, sine, cosine)
    out_sine = jnp.where((quadrant & 2) == 2, -out_sine, out_sine)
    out_cosine = jnp.where(((quadrant + 1) & 2) == 2, -out_cosine, out_cosine)
    return out_sine, out_cosine


def march_kernel(
    n, steps, factors, cap, halo,
    field_hbm, brick_hbm, index_hbm, count_hbm, weights_hbm, prop_ref,
    out_ref,
    field_ref, brick_ref, index_ref, count_ref, weights_ref,
    prop, step_prop, rows_f, picks, packed, recv, mixw, angles,
    fpeer_s, fpeer_r, fhalo_s, fhalo_r,
    apeer_s, apeer_r, ahalo_s, ahalo_r,
    sines, cosines, state, stencil,
    load_sem, brick_sem, prop_sem, pp_ss, pp_rs, a2a_ss, a2a_rs, fp_sem, fh_ss, fh_rs, ap_ss, ap_rs, ah_ss, ah_rs,
):
    i = lax.axis_index("az")
    j = lax.axis_index("dep")
    other = 1 - j
    rows = weights_ref.shape[0]
    whole = prop.shape[2]
    block_rows = LANES
    share = lax.rem(i, 2)
    twin = i + 1 - 2 * share
    window = rows + 2 * halo
    chunks = packed.shape[0]
    depth = chunks * LANES
    bcol = brick_ref.shape[1]
    before = lax.rem(i + n - 1, n)
    after = lax.rem(i + 1, n)
    deps = (j, other)

    barrier = pltpu.get_barrier_semaphore()

    loads = []

    def load(src, dst):
        copy = pltpu.make_async_copy(src, dst, load_sem.at[len(loads)])
        copy.start()
        loads.append(copy)

    load(index_hbm, index_ref)
    load(count_hbm, count_ref)
    bricks = []
    for c in range(chunks):
        copy = pltpu.make_async_copy(
            brick_hbm.at[:, pl.ds(c * LANES, LANES)], brick_ref.at[c], brick_sem.at[c]
        )
        copy.start()
        bricks.append(copy)

    def greet(q, carry):
        pl.semaphore_signal(
            barrier, inc=1, device_id=(lax.rem(i + 1 + q, n), j), device_id_type=MESH
        )
        return carry

    lax.fori_loop(0, n - 1, greet, 0)
    for target in (i, before, after):
        pl.semaphore_signal(barrier, inc=1, device_id=(target, other), device_id_type=MESH)

    load(field_hbm, field_ref)
    load(weights_hbm, weights_ref)
    fetches = []
    for f in range(factors):
        fetch = pltpu.make_async_copy(prop_ref.at[f], prop.at[f], prop_sem.at[f])
        fetch.start()
        fetches.append(fetch)

    for copy in loads[0:2]:
        copy.wait()
    slots = lax.broadcasted_iota(jnp.int32, (cap, n), 0)
    chosen = jnp.transpose(index_ref[0], (1, 0))
    chosen = jnp.where(slots < count_ref[...], chosen, -1)
    column = lax.broadcasted_iota(jnp.int32, (cap, bcol), 1)
    group = min(n, 8)
    for d in range(n):
        picks[d * cap : (d + 1) * cap, :] = (
            (column == chosen[:, d : d + 1]).astype(jnp.float32).astype(jnp.bfloat16)
        )

    def pick(c):
        bricks[c].wait()
        for g in range(n // group):
            picked = jnp.dot(
                picks[g * group * cap : (g + 1) * group * cap, :], brick_ref[c],
                preferred_element_type=jnp.float32,
            )
            packed[c, g * group : (g + 1) * group] = picked.astype(jnp.bfloat16).reshape(
                group, cap, LANES
            )

    pick(0)
    pl.semaphore_wait(barrier, n + 2)

    planes = 4 if n % 4 == 0 else 1
    plane = n // planes
    mine = lax.div(i, plane)
    spot = lax.rem(i, plane)
    if planes == 4:
        upper = lax.div(mine, 2)
        order = (3 - 3 * upper, 2 - upper, mine + 1 - 2 * lax.rem(mine, 2), mine)
    else:
        order = (mine,)

    def send(c, target):
        pltpu.make_async_remote_copy(
            src_ref=packed.at[c, target],
            dst_ref=recv.at[c, i],
            send_sem=a2a_ss.at[0],
            recv_sem=a2a_rs.at[c],
            device_id=(target, j),
            device_id_type=MESH,
        ).start()

    def send_last(c):
        @pl.when(i != n - 1)
        def _():
            send(c, n - 1)

    def send_all(c):
        for p, there in enumerate(order):
            own = p == planes - 1

            def spread(q, carry, there=there, own=own):
                target = there * plane + lax.rem(spot + q + own, plane)

                @pl.when(target != n - 1)
                def _():
                    send(c, target)

                return carry

            lax.fori_loop(0, plane - own, spread, 0)

    send_last(0)
    send_all(0)
    for c in range(1, chunks):
        for ahead in (2 * c - 1, 2 * c):
            if ahead < chunks:
                pick(ahead)
                send_last(ahead)
        send_all(c)
    for c in range(chunks):
        recv[c, i] = packed[c, i]

    loads[2].wait()

    def strided(ref, start, stride):
        return jnp.concatenate(
            [ref[c, pl.ds(start, rows, stride=stride), :] for c in range(ref.shape[0])], axis=1
        )

    def field_part(p):
        return jnp.concatenate(
            [
                field_ref[pl.ds(2 * c + p, rows, stride=2 * chunks), :]
                for c in range(chunks)
            ],
            axis=1,
        )

    parts = [field_part(p) for p in range(2)]
    for p in range(2):
        fpeer_s[p] = parts[p].astype(jnp.bfloat16)
    fhalo_s[0] = jnp.concatenate([parts[0][0:halo], parts[1][0:halo]], axis=0).astype(jnp.bfloat16)
    fhalo_s[1] = jnp.concatenate(
        [parts[0][rows - halo : rows], parts[1][rows - halo : rows]], axis=0
    ).astype(jnp.bfloat16)

    def remote(src, dst, send_sem, recv_sem, target):
        return pltpu.make_async_remote_copy(
            src_ref=src, dst_ref=dst, send_sem=send_sem, recv_sem=recv_sem,
            device_id=target, device_id_type=MESH,
        )

    def local_wait(ref, sem):
        pltpu.make_async_copy(ref, ref, sem).wait()

    def launch(src, dst, send_sem, recv_sem, target):
        remote(src, dst, send_sem, recv_sem, target).start()

    launch(fpeer_s, fpeer_r, fp_sem.at[0], fp_sem.at[1], (i, other))
    for t, dep in enumerate(deps):
        launch(fhalo_s.at[0], fhalo_r.at[1, j], fh_ss.at[t], fh_rs.at[0], (before, dep))
        launch(fhalo_s.at[1], fhalo_r.at[0, j], fh_ss.at[t], fh_rs.at[0], (after, dep))

    loads[3].wait()
    for a in range(rows):
        block = weights_ref[a].astype(jnp.float32)
        for c in range(n * cap // LANES):
            rows_f[c, steps * a : steps * (a + 1), :] = block[:, c * LANES : (c + 1) * LANES]
    for k in range(steps):
        mixw[k * rows : (k + 1) * rows, :] = strided(rows_f, k, steps).astype(jnp.bfloat16)

    def windowed(low, body, high):
        return jnp.concatenate([low, body, high], axis=0)

    def finish(c, k):
        cols = pl.ds(c * LANES, LANES)
        for side in deps:
            body = angles[c, k] if side is j else apeer_r[c, k].astype(jnp.float32)
            low = ahalo_r[c, 0, side, k].astype(jnp.float32)
            high = ahalo_r[c, 1, side, k].astype(jnp.float32)
            s, co = sine_cosine(windowed(low, body, high))
            sines[k, side, :, cols] = s
            cosines[k, side, :, cols] = co

    def operand(re, im):
        re = re.astype(jnp.bfloat16)
        im = im.astype(jnp.bfloat16)
        left = jnp.concatenate([re, im], axis=0)
        right = jnp.concatenate([-im, re], axis=0)
        return jnp.concatenate([left, right], axis=1)

    def compose(b):
        at = pl.multiple_of(share * (whole // 2) + b * block_rows, block_rows)
        span = pl.ds(at, block_rows)
        re = prop[0, span, :]
        im = prop[0, pl.ds(whole + at, block_rows), :]
        for f in range(1, factors):
            mixed = jnp.dot(operand(re, im), prop[f], preferred_element_type=jnp.float32)
            re, im = mixed[0:block_rows], mixed[block_rows : 2 * block_rows]
        step_prop[0, span, :] = re.astype(jnp.bfloat16)
        step_prop[1, span, :] = im.astype(jnp.bfloat16)
        piece = step_prop.at[:, span, :]
        remote(piece, piece, pp_ss.at[0], pp_rs.at[0], (twin, j)).start()

    for fetch in fetches:
        fetch.wait()
    blocks = whole // 2 // LANES
    early = max(chunks - 2, 0)
    for c in range(chunks):
        for b in range(min(c * blocks // 2, blocks), min((c + 1) * blocks // 2, blocks)):
            compose(b)
        local_wait(recv.at[c, pl.ds(0, n - 1)], a2a_rs.at[c])
        flat = recv[c].reshape(n * cap, LANES)
        speed = jnp.dot(mixw[...], flat, preferred_element_type=jnp.float32)
        angle = -angle_rate * speed
        for k in range(steps):
            x = angle[k * rows : (k + 1) * rows]
            angles[c, k] = x
            apeer_s[c, k] = x.astype(jnp.bfloat16)
            ahalo_s[c, 0, k] = x[0:halo].astype(jnp.bfloat16)
            ahalo_s[c, 1, k] = x[rows - halo : rows].astype(jnp.bfloat16)
        group = int(c >= early)

        def exchange_edges():
            for t, dep in enumerate(deps):
                launch(
                    ahalo_s.at[c, 0], ahalo_r.at[c, 1, j], ah_ss.at[t], ah_rs.at[group],
                    (before, dep),
                )
                launch(
                    ahalo_s.at[c, 1], ahalo_r.at[c, 0, j], ah_ss.at[t], ah_rs.at[group],
                    (after, dep),
                )

        if c < early:
            wanted = [(c, k) for k in range(steps)]
        elif c < chunks - 1:
            wanted = [(c, k) for k in range(steps // 2)]
        else:
            wanted = [
                (b, k) for k in range(steps) for b in range(early, chunks)
                if b == c or k >= steps // 2
            ]
        for q, (b, k) in enumerate(wanted):
            launch(
                apeer_s.at[b, k], apeer_r.at[b, k], ap_ss.at[0],
                ap_rs.at[0 if b < early else 1 + k], (i, other),
            )
            if q == 0:
                exchange_edges()
    local_wait(fpeer_r, fp_sem.at[1])
    local_wait(fhalo_r, fh_rs.at[0])
    for side in deps:
        lows = fhalo_r[0, side].astype(jnp.float32)
        highs = fhalo_r[1, side].astype(jnp.float32)
        for p in range(2):
            if side is j:
                part = field_part(p).astype(jnp.bfloat16).astype(jnp.float32)
            else:
                part = fpeer_r[p].astype(jnp.float32)
            span = slice(p * halo, (p + 1) * halo)
            state[p, side] = windowed(lows[span], part, highs[span])
    if early:
        local_wait(apeer_r.at[pl.ds(0, early)], ap_rs.at[0])
        local_wait(ahalo_r.at[pl.ds(0, early)], ah_rs.at[0])
    for c in range(early):
        for k in range(steps):
            finish(c, k)
    local_wait(ahalo_r.at[pl.ds(early, chunks - early)], ah_rs.at[1])

    def arrive(k):
        local_wait(apeer_r.at[pl.ds(early, chunks - early), k], ap_rs.at[1 + k])

    def settle(k):
        for c in range(early, chunks):
            finish(c, k)

    def half_prop(which):
        at = pl.multiple_of(which * (whole // 2), LANES)
        return step_prop.at[:, pl.ds(at, whole // 2), :]

    local_wait(half_prop(1 - share), pp_rs.at[0])
    across = lax.broadcasted_iota(jnp.int32, (window, window), 0)
    gap = across - lax.broadcasted_iota(jnp.int32, (window, window), 1)
    near = jnp.where((gap == 1) | (gap == -1), 16.0, jnp.where((gap == 2) | (gap == -2), -1.0, 0.0))
    stencil[...] = jnp.where(gap == 0, -30.0, near).astype(jnp.bfloat16)

    def laplace(x):
        return jnp.dot(stencil[...], x.astype(jnp.bfloat16), preferred_element_type=jnp.float32)

    def couple(k):
        tops, lows = [], []
        for side in range(2):
            re, im = state[0, side], state[1, side]
            co, si = cosines[k, side], sines[k, side]
            sre = re * co - im * si
            sim = re * si + im * co
            lre, lim = laplace(sre), laplace(sim)
            tops.append(sre + (couple_real / 12.0) * lre - (couple_imag / 12.0) * lim)
            lows.append(sim + (couple_real / 12.0) * lim + (couple_imag / 12.0) * lre)
        return jnp.concatenate(tops, axis=1), jnp.concatenate(lows, axis=1)

    def march(k, carry):
        re, im = couple(k)
        both = operand(re, im)
        arrive(k + 1)
        mixed = jnp.dot(both, step_prop[...].reshape(2 * whole, whole), preferred_element_type=jnp.float32)
        settle(k + 1)
        re, im = mixed[0:window], mixed[window : 2 * window]
        for side in range(2):
            state[0, side] = re[:, side * depth : (side + 1) * depth]
            state[1, side] = im[:, side * depth : (side + 1) * depth]
        return carry

    arrive(0)
    settle(0)
    lax.fori_loop(0, steps - 1, march, 0)

    re, im = couple(steps - 1)
    inner = slice(halo, halo + rows)
    both = operand(re[inner], im[inner])
    columns = pl.ds(pl.multiple_of(j * depth, LANES), depth)
    mixed = jnp.dot(
        both, step_prop[:, :, columns].reshape(2 * whole, depth), preferred_element_type=jnp.float32
    )
    for p in range(2):
        for c in range(chunks):
            out_ref[pl.ds(2 * c + p, rows, stride=2 * chunks), :] = mixed[
                p * rows : (p + 1) * rows, c * LANES : (c + 1) * LANES
            ]

    local_wait(packed.at[:, pl.ds(0, n - 1)], a2a_ss.at[0])
    local_wait(fpeer_s, fp_sem.at[0])
    local_wait(half_prop(share), pp_ss.at[0])
    local_wait(apeer_s, ap_ss.at[0])
    for t in range(2):
        local_wait(fhalo_s, fh_ss.at[t])
        local_wait(ahalo_s, ah_ss.at[t])


def per_device(field, brick_speed, send_index, send_count, weights, propagator):
    n = lax.axis_size("az")
    rows, _, depth = field.shape
    steps = weights.shape[1]
    factors, _, whole, _ = propagator.shape
    cap = send_index.shape[2]
    halo = 2 * steps
    window = rows + 2 * halo
    chunks = depth // LANES
    merged = propagator.reshape(factors, 2 * whole, whole)
    flat_field = field.reshape(rows, 2, chunks, LANES).transpose(0, 2, 1, 3).reshape(-1, LANES)
    bf16, f32 = jnp.bfloat16, jnp.float32
    dma = pltpu.SemaphoreType.DMA
    vmem = pl.BlockSpec(memory_space=pltpu.VMEM)
    out = pl.pallas_call(
        functools.partial(march_kernel, n, steps, factors, cap, halo),
        out_shape=pltpu.VMEM(flat_field.shape, f32),
        in_specs=[pl.BlockSpec(memory_space=pl.ANY)] * 6,
        out_specs=vmem,
        scratch_shapes=[
            pltpu.VMEM(flat_field.shape, f32),
            pltpu.VMEM((chunks, brick_speed.shape[0], LANES), bf16),
            pltpu.VMEM(send_index.shape, jnp.int32),
            pltpu.VMEM(send_count.shape, jnp.int32),
            pltpu.VMEM(weights.shape, bf16),
            pltpu.VMEM((factors, 2 * whole, whole), bf16),
            pltpu.VMEM((2, whole, whole), bf16),
            pltpu.VMEM((n * cap // LANES, rows * steps, LANES), f32),
            pltpu.VMEM((n * cap, brick_speed.shape[0]), bf16),
            pltpu.VMEM((chunks, n, cap, LANES), bf16),
            pltpu.VMEM((chunks, n, cap, LANES), bf16),
            pltpu.VMEM((rows * steps, n * cap), bf16),
            pltpu.VMEM((chunks, steps, rows, LANES), f32),
            pltpu.VMEM((2, rows, depth), bf16),
            pltpu.VMEM((2, rows, depth), bf16),
            pltpu.VMEM((2, 2 * halo, depth), bf16),
            pltpu.VMEM((2, 2, 2 * halo, depth), bf16),
            pltpu.VMEM((chunks, steps, rows, LANES), bf16),
            pltpu.VMEM((chunks, steps, rows, LANES), bf16),
            pltpu.VMEM((chunks, 2, steps, halo, LANES), bf16),
            pltpu.VMEM((chunks, 2, 2, steps, halo, LANES), bf16),
            pltpu.VMEM((steps, 2, window, depth), f32),
            pltpu.VMEM((steps, 2, window, depth), f32),
            pltpu.VMEM((2, 2, window, depth), f32),
            pltpu.VMEM((window, window), bf16),
            dma((4,)),
            dma((chunks,)),
            dma((factors,)),
            dma((1,)),
            dma((1,)),
            dma((1,)),
            dma((chunks,)),
            dma((2,)),
            dma((2,)),
            dma((1,)),
            dma((1,)),
            dma((1 + steps,)),
            dma((2,)),
            dma((2,)),
        ],
        compiler_params=pltpu.CompilerParams(collective_id=0, has_side_effects=True),
    )(flat_field, brick_speed, send_index, send_count, weights, merged)
    return out.reshape(rows, chunks, 2, LANES).transpose(0, 2, 1, 3).reshape(rows, 2, depth)


def solution(mesh):
    placed = (
        P("az", None, "dep"),
        P("az", "dep"),
        P("az", None, None),
        P("az", None),
        P("az", None, None),
        P(),
    )
    return jax.shard_map(
        per_device, mesh=mesh, in_specs=placed, out_specs=P("az", None, "dep"), check_vma=False
    )
```

time: 31.4 us -> 29.4 us (0.936)
  Pallas kernels: 30.5 us -> 28.6 us
    pallas_call x1, Pallas kernels: 30.5 us -> 28.6 us  [per_device(): pl.pallas_call(functools.partial(march_kernel, n, steps, factors, cap, ha...]
where the time goes in v2:
time: 29.4 us; the launch traced here: 29.3 us
  Pallas kernels  28.6 us (97%)
  local copies, waits for them, and re-layouts  0.71 us (2%)
    pallas_call x1, Pallas kernels, per_device(): pl.pallas_call(functools.partial(march_kernel, n, steps, factors, cap, ha...  28.6 us
    unnamed x1, local copies, waits for them, and re-layouts  0.71 us

profile of v2, /device:TPU:0, one launch (start us, length us, event | category | flops | bytes accessed | tf_op | source)
XLA Modules:
  0.0 29.3 jit_solution(11164572013529891844)
XLA Ops:
  0.0 28.6 %shard_map.64 = f32[512,128]{1,0:T(8,128)S(1)} custom-call(f32[512,128]{1,0:T(8,128)} %bitcast.13, bf16[256,512]{1,0:T(8,128)(2,1)} %brick_hbm.1, s32[1,16,32]{2,1,0:T(8,128)} %index_hbm.1, s32[1,16]{1,0:T(1,128)} %count_hbm.1, bf16[64,4,512]{2,1,0:T(4,128)(2,1)} %weights_hbm.1, bf16[2,2048,1024]{2,1,0:T(8,128)(2,1)} %bitcast.12), custom_call_target="tpu_custom_call" | custom-call | tf_op jit(solution)/shard_map/pallas_call | solution.py:408
  28.6 0.7 %copy.10 = f32[64,2,512]{2,1,0:T(2,128)} copy(f32[64,2,512]{2,1,0:T(2,128)S(1)} %bitcast.11) | data formatting | bytes 524288
